TPU v7x, 256 devices: a whole 4x4x8 slice. The times are simulated.
256 devices in a mesh: row: 16 (over x_hi, z), blk: 16 (over x_lo, y, core).
Axes of the slice: x: 4 (x_hi: 2, x_lo: 2; x = x_hi * 2 + x_lo), y: 4, z: 8, core: 2. Of those that a mesh axis runs over, the one named last changes fastest.
Arguments:
- source_table: bfloat16 [8192, 512], P('blk'), may hold values from -6 to 6
- target_table: bfloat16 [131072, 512], P(('row', 'blk')), may hold values from -6 to 6
- message_weight: bfloat16 [512, 512], replicated, may hold values from -0.25 to 0.25
- self_weight: bfloat16 [512, 512], replicated, may hold values from -0.25 to 0.25
- tile_lists: int32 [256, 16], P(('row', 'blk')), may hold values from 0 to 15, each once within a row
- key_offsets: int32 [131072, 16], P(('row', 'blk')), may hold values from 0 to 511
- list_lengths: int32 [256], P(('row', 'blk')), may hold values from 1 to 16, 2048 in all
- cotangent: bfloat16 [131072, 512], P(('row', 'blk')), may hold values from -6 to 6
Outputs:
- updated: bfloat16 [131072, 512], P(('row', 'blk'))
- target_gradient: bfloat16 [131072, 512], P(('row', 'blk'))
- source_gradient: bfloat16 [8192, 512], P(('blk', 'row'))
- self_gradient: float32 [512, 512], replicated
- message_gradient: float32 [512, 512], replicated
Inputs may be any that keep to these rules, and one draw needn't show every extreme that they name: Each row of tile_lists names every one of the 16 source tiles once. A target tile uses the first list_lengths entries of its row of tile_lists.
All inputs are finite; a program needn't handle non-finite values. No bound on the sum of `list_lengths` on one device may be relied on, other than what follows from the above.
Results may differ from a plain program's by a relative error of at most 0.0058.
Values may be sent and summed in bfloat16 or wider, within the bound.
A program may use at most 64 MiB of HBM per device.

v0:
```python
import jax
import jax.numpy as jnp
from jax import lax
from jax.sharding import PartitionSpec as P


def slot_table(lists):
    slot_count = lists.shape[1]
    slot_ids = lax.iota(jnp.int32, slot_count)
    matches = lists[:, :, None] == slot_ids[None, None, :]
    return jnp.sum(jnp.where(matches, slot_ids[None, :, None], 0), axis=1)


def tile_patterns(offset_tiles, slot_column, lengths, tile_rows):
    slot_count = offset_tiles.shape[2]
    chosen_slot = lax.iota(jnp.int32, slot_count)[None, None, :] == slot_column[:, None, None]
    chosen = jnp.sum(jnp.where(chosen_slot, offset_tiles, 0), axis=2)
    used = slot_column < lengths
    positions = lax.iota(jnp.int32, tile_rows)
    pattern = (chosen[:, :, None] == positions[None, None, :]) & used[:, None, None]
    return pattern.astype(jnp.bfloat16)


def local(
    source_table,
    target_table,
    message_weight,
    self_weight,
    tile_lists,
    key_offsets,
    list_lengths,
    cotangent,
):
    tile_rows = target_table.shape[0] // tile_lists.shape[0]
    tiles_here = tile_lists.shape[0]
    slot_count = tile_lists.shape[1]
    width = target_table.shape[1]
    block_rows = source_table.shape[0]
    row_devices = lax.axis_size("row")
    share_rows = block_rows // row_devices
    own_rows = lax.dynamic_slice_in_dim(
        source_table, lax.axis_index("row") * share_rows, share_rows, 0
    )
    projected = jnp.dot(source_table, message_weight, preferred_element_type=jnp.float32).astype(
        jnp.bfloat16
    )
    inverse_tile = 1.0 / list_lengths.astype(jnp.float32)
    slot_of = slot_table(tile_lists)
    offset_tiles = key_offsets.reshape(tiles_here, tile_rows, slot_count)
    start_sum = jnp.zeros((target_table.shape[0], width), jnp.float32)
    pieces = lax.all_gather(projected, "blk", axis=0, tiled=True)
    piece_tiles = pieces.shape[0] // tile_rows

    def gather_visit(local_tile, running):
        source_tile = lax.dynamic_slice_in_dim(pieces, local_tile * tile_rows, tile_rows, 0)
        slot_column = lax.dynamic_index_in_dim(slot_of, local_tile, 1, keepdims=False)
        pattern = tile_patterns(offset_tiles, slot_column, list_lengths, tile_rows)
        added = jnp.einsum("trc,cw->trw", pattern, source_tile, preferred_element_type=jnp.float32)
        return running + added.reshape(running.shape)

    gathered = lax.fori_loop(0, piece_tiles, gather_visit, start_sum)
    inverse_row = jnp.repeat(inverse_tile, tile_rows)[:, None]
    preact = (
        jnp.dot(target_table, self_weight, preferred_element_type=jnp.float32)
        + gathered * inverse_row
    )
    sigmoid_pre = jax.nn.sigmoid(preact)
    updated = (target_table.astype(jnp.float32) + preact * sigmoid_pre).astype(jnp.bfloat16)
    upstream = cotangent.astype(jnp.float32)
    grad_pre = (upstream * sigmoid_pre * (1.0 + preact * (1.0 - sigmoid_pre))).astype(jnp.bfloat16)
    target_gradient = (
        upstream + jnp.dot(grad_pre, self_weight.T, preferred_element_type=jnp.float32)
    ).astype(jnp.bfloat16)
    grad_tiles = grad_pre.reshape(tiles_here, tile_rows, width)

    def tile_terms(slot_column, offsets, lengths, inverses, grads):
        pattern = tile_patterns(offsets, slot_column, lengths, tile_rows)
        terms = jnp.einsum("trc,trw->tcw", pattern, grads, preferred_element_type=jnp.float32)
        return jnp.sum(terms * inverses[:, None, None], axis=0)

    def partial_visit(local_tile, running):
        slot_column = lax.dynamic_index_in_dim(slot_of, local_tile, 1, keepdims=False)
        term = tile_terms(slot_column, offset_tiles, list_lengths, inverse_tile, grad_tiles)
        return lax.dynamic_update_slice_in_dim(running, term, local_tile * tile_rows, 0)

    block_sum = lax.psum_scatter(
        lax.fori_loop(
            0,
            block_rows * lax.axis_size("blk") // tile_rows,
            partial_visit,
            jnp.zeros((block_rows * lax.axis_size("blk"), width), jnp.float32),
        ),
        "blk",
        scatter_dimension=0,
        tiled=True,
    )
    source_sum = lax.psum_scatter(block_sum, "row", scatter_dimension=0, tiled=True)
    source_grad_rounded = source_sum.astype(jnp.bfloat16)
    source_gradient = jnp.dot(
        source_grad_rounded, message_weight.T, preferred_element_type=jnp.float32
    ).astype(jnp.bfloat16)
    self_partial = jnp.dot(target_table.T, grad_pre, preferred_element_type=jnp.float32)
    message_partial = jnp.dot(own_rows.T, source_grad_rounded, preferred_element_type=jnp.float32)
    self_total, message_total = lax.psum((self_partial, message_partial), ("row", "blk"))
    target_total = target_table.shape[0] * row_devices * lax.axis_size("blk")
    source_total = block_rows * lax.axis_size("blk")
    self_gradient = self_total * target_total ** (-0.5)
    message_gradient = message_total * source_total ** (-0.5)
    return (updated, target_gradient, source_gradient, self_gradient, message_gradient)


def solution(mesh):
    placed = (
        P("blk", None),
        P(("row", "blk"), None),
        P(),
        P(),
        P(("row", "blk"), None),
        P(("row", "blk"), None),
        P(("row", "blk")),
        P(("row", "blk"), None),
    )
    return jax.shard_map(
        local,
        mesh=mesh,
        in_specs=placed,
        out_specs=(
            P(("row", "blk"), None),
            P(("row", "blk"), None),
            P(("blk", "row"), None),
            P(),
            P(),
        ),
        check_vma=False,
    )
```

profile of v0, /device:TPU:2, one launch (start us, length us, event | category | flops | bytes accessed | tf_op | source)
XLA Modules:
  0.0 807.8 jit_solution(3190670035176118978)
XLA Ops:
  7.2 2.5 convolution_convert_fusion
  11.2 56.8 %all-gather.2.cloned.1.call-done = bf16[8192,512]{1,0:T(8,128)(2,1)} async-done(((bf16[512,512]{1,0:T(8,128)(2,1)}), bf16[8192,512]{1,0:T(8,128)(2,1)}) %all-gather.2.cloned.1.call-update) | async-done | bytes 8388624 | tf_op jit(solution)/shard_map/all_gather | solution.py:51
  68.0 80.6 %while.28 = (s32[]{:T(128)}, f32[512,512]{1,0:T(8,128)S(1)}, s32[1,16]{1,0:T(1,128)S(1)}, s32[1,512,16]{1,2,0:T(8,128)}, s32[1]{0:T(128)}, /*index=5*/bf16[8192,...) while((s32[]{:T(128)}, f32[512,512]{1,0:T(8,128)S(1)}, s32[1,16]{1,0:T(1,128)S(1)}, ...), condition=%wide.region_3.4_spmd.clone, body=%wide.region_1.3_spmd.clone.sunk | while | flops 269499936 | bytes 2659034 | solution.py:61
  71.4 1.6 convolution_add_fusion.4
  76.4 1.6 convolution_add_fusion.4
  86.5 1.6 convolution_add_fusion.4
  91.6 1.6 convolution_add_fusion.4
  96.6 1.6 convolution_add_fusion.4
  101.6 1.6 convolution_add_fusion.4
  106.7 1.6 convolution_add_fusion.4
  116.8 1.6 convolution_add_fusion.4
  121.8 1.6 convolution_add_fusion.4
  131.9 1.6 convolution_add_fusion.4
  136.9 1.6 convolution_add_fusion.4
  147.0 1.6 convolution_add_fusion.4
  148.7 3.0 fusion.15
  151.7 7.9 broadcast_in_dim.94
  159.6 67.2 %while.27 = (s32[]{:T(128)}, f32[8192,512]{1,0:T(8,128)}, s32[1,16]{1,0:T(1,128)S(1)}, s32[1,512,16]{1,2,0:T(8,128)S(1)}, s32[1]{0:T(128)}, /*index=5*/bf16[1,51...) while((s32[]{:T(128)}, f32[8192,512]{1,0:T(8,128)}, ...), condition=%wide.region_6.7_spmd, body=%wide.region_4.6_spmd.sunk | while | flops 269237792 | bytes 1610968 | solution.py:87
  226.8 101.1 %reduce-scatter.3.cloned.1.call-done = f32[512,512]{1,0:T(8,128)} async-done(((f32[8192,512]{1,0:T(8,128)}), f32[512,512]{1,0:T(8,128)}) %reduce-scatter.3.cloned.1.call-update) | async-done | bytes 1048592 | tf_op jit(solution)/shard_map/reduce_scatter | solution.py:86
  329.4 200.2 %reduce-scatter.5.cloned.1.call-done = f32[32,512]{1,0:T(8,128)} async-done(((f32[512,512]{1,0:T(8,128)}), f32[32,512]{1,0:T(8,128)}) %reduce-scatter.5.cloned.1.call-update) | async-done | bytes 65552 | tf_op jit(solution)/shard_map/reduce_scatter | solution.py:97
  529.6 2.1 fusion.16
  533.1 1.7 convolution_convert_fusion.1
  534.8 261.5 %all-reduce.3.cloned.1.call-done = (f32[512,512]{0,1:T(8,128)}, f32[512,512]{1,0:T(8,128)}) async-done(((f32[512,512]{0,1:T(8,128)}, f32[512,512]{1,0:T(8,128)}), (f32[512,512]{0,1:T(8,128)}, f32[512,512]{1,0:T(8,128)})) %all-reduce.3.cloned.1.call-update) | async-done | bytes 2097168 | tf_op jit(solution)/shard_map/psum | solution.py:104
  799.0 2.3 broadcast_multiply_fusion
  (140 shorter events, 92.3 us)
Async XLA Ops:
  7.2 141.5 %copy-start = (bf16[512,512]{1,0:T(8,128)(2,1)S(1)}, bf16[512,512]{1,0:T(8,128)(2,1)}, u32[]{:S(2)}) copy-start(bf16[512,512]{1,0:T(8,128)(2,1)} %param.15) | copy-start | bytes 1572868
  7.2 60.8 %all-gather.2.cloned.1.call-start = ((), (), s32[]{:S(2)}) async-start(), calls=%async_computation.2 | async-start | bytes 8912896 | tf_op jit(solution)/shard_map/all_gather | solution.py:51
  9.7 318.2 %reduce-scatter.3.cloned.1.call-start = ((), (), s32[]{:S(2)}) async-start(), calls=%async_computation.3 | async-start | bytes 17825792 | tf_op jit(solution)/shard_map/reduce_scatter | solution.py:86
  148.6 10.9 %copy-start.1 = (s32[1,512,16]{1,2,0:T(8,128)S(1)}, s32[1,512,16]{1,2,0:T(8,128)}, u32[]{:S(2)}) copy-start(s32[1,512,16]{1,2,0:T(8,128)} %get-tuple-element.461) | copy-start | bytes 98308
  159.6 168.4 %copy-start.3 = (bf16[512,512]{1,0:T(8,128)(2,1)S(1)}, bf16[512,512]{1,0:T(8,128)(2,1)}, u32[]{:S(2)}) copy-start(bf16[512,512]{1,0:T(8,128)(2,1)} %param.13) | copy-start | bytes 1572868
  159.6 372.2 %copy-start.4 = (bf16[512,512]{1,0:T(8,128)(2,1)S(1)}, bf16[512,512]{1,0:T(8,128)(2,1)}, u32[]{:S(2)}) copy-start(bf16[512,512]{1,0:T(8,128)(2,1)} %param.19) | copy-start | bytes 1572868
  159.6 373.5 %copy-start.2 = (bf16[512,512]{1,0:T(8,128)(2,1)S(1)}, bf16[512,512]{1,0:T(8,128)(2,1)}, u32[]{:S(2)}) copy-start(bf16[512,512]{1,0:T(8,128)(2,1)} %param.14) | copy-start | bytes 1572868
  226.8 302.9 %reduce-scatter.5.cloned.1.call-start = ((), (), s32[]{:S(2)}) async-start(), calls=%async_computation.4 | async-start | bytes 1114112 | tf_op jit(solution)/shard_map/reduce_scatter | solution.py:97
  327.9 468.4 %all-reduce.3.cloned.1.call-start = ((), (), s32[]{:S(2)}) async-start(), calls=%async_computation.5 | async-start | bytes 4194304 | tf_op jit(solution)/shard_map/psum | solution.py:104
Sparse Core Ops, SparseCore 0:
  10.4 57.5 all-gather.1
  226.9 100.9 reduce-scatter.2
  331.7 197.8 reduce-scatter.4
  535.6 260.6 all-reduce.2
where the time goes:
time: 811 us; the launch traced here: 808 us
  waiting for transfers between devices  620 us (76%)
  matrix products  63 us (8%)
  loops' own time  42.4 us (5%)
  other arithmetic  40.2 us (5%)
  local copies, waits for them, and re-layouts  27.9 us (3%)
  between operations  14.5 us (2%)
    psum x1, waiting for transfers between devices, local(): lax.psum((self_partial, message_partial), ('row', 'blk'))  262 us
    reduce_scatter x1, waiting for transfers between devices, local(): lax.psum_scatter(block_sum, 'row', scatter_dimension=0, tiled=True)  200 us
    reduce_scatter x1, waiting for transfers between devices, local(): lax.psum_scatter(lax.fori_loop(0, block_rows * lax.axis_size('blk') // ti...  101 us
    all_gather x1, waiting for transfers between devices, local(): pieces = lax.all_gather(projected, 'blk', axis=0, tiled=True)  56.8 us
    dot_general x16, matrix products, gather_visit(): jnp.einsum('trc,cw->trw', pattern, source_tile, preferred_element_type=jn...  25.9 us
    dot_general x16, matrix products, tile_terms(): jnp.einsum('trc,trw->tcw', pattern, grads, preferred_element_type=jnp.flo...  25.1 us
    another operation x1, loops' own time, local(): gathered = lax.fori_loop(0, piece_tiles, gather_visit, start_sum)  21.4 us
    another operation x1, loops' own time, local(): lax.fori_loop(0, block_rows * lax.axis_size('blk') // tile_rows, partial_...  21 us
  transfers between devices with their start and end apart: 4, of which 4 were waited for; matrix products, arithmetic and copies ran while one was open for 1% of the time, Pallas kernels for 0%

commit v1 on v0

--- a/solution.py
+++ b/solution.py
@@ -2,6 +2,11 @@
 import jax.numpy as jnp
 from jax import lax
 from jax.sharding import PartitionSpec as P
+
+
+def by_each_axis(x, one, other):
+    half = lax.psum(x, one)
+    return lax.psum(half, other)
 
 
 def slot_table(lists):
@@ -101,7 +106,7 @@
     ).astype(jnp.bfloat16)
     self_partial = jnp.dot(target_table.T, grad_pre, preferred_element_type=jnp.float32)
     message_partial = jnp.dot(own_rows.T, source_grad_rounded, preferred_element_type=jnp.float32)
-    self_total, message_total = lax.psum((self_partial, message_partial), ("row", "blk"))
+    self_total, message_total = by_each_axis((self_partial, message_partial), "row", "blk")
     target_total = target_table.shape[0] * row_devices * lax.axis_size("blk")
     source_total = block_rows * lax.axis_size("blk")
     self_gradient = self_total * target_total ** (-0.5)

time: 811 us -> 838 us (1.033)
  waiting for transfers between devices: 620 us -> 646 us
    psum x1 -> x2, waiting for transfers between devices: 262 us -> 288 us  [the longest x1 162 us: by_each_axis(): half = lax.psum(x, one)]
  transfers between devices with their start and end apart: 4 -> 5, of which waited for: 4 -> 5; matrix products, arithmetic and copies ran while one was open for 1% -> 1% of each run, Pallas kernels for 0% -> 0%
where the time goes in v1:
time: 838 us; the launch traced here: 834 us
  waiting for transfers between devices  646 us (77%)
  matrix products  63.2 us (8%)
  loops' own time  42.4 us (5%)
  other arithmetic  40.2 us (5%)
  local copies, waits for them, and re-layouts  27.9 us (3%)
  between operations  14.5 us (2%)
    reduce_scatter x1, waiting for transfers between devices, local(): lax.psum_scatter(block_sum, 'row', scatter_dimension=0, tiled=True)  200 us
    psum x1, waiting for transfers between devices, by_each_axis(): half = lax.psum(x, one)  162 us
    psum x1, waiting for transfers between devices, by_each_axis(): return lax.psum(half, other)  125 us
    reduce_scatter x1, waiting for transfers between devices, local(): lax.psum_scatter(lax.fori_loop(0, block_rows * lax.axis_size('blk') // ti...  101 us
    all_gather x1, waiting for transfers between devices, local(): pieces = lax.all_gather(projected, 'blk', axis=0, tiled=True)  56.8 us
    dot_general x16, matrix products, gather_visit(): jnp.einsum('trc,cw->trw', pattern, source_tile, preferred_element_type=jn...  25.9 us
    dot_general x16, matrix products, tile_terms(): jnp.einsum('trc,trw->tcw', pattern, grads, preferred_element_type=jnp.flo...  25.2 us
    another operation x1, loops' own time, local(): gathered = lax.fori_loop(0, piece_tiles, gather_visit, start_sum)  21.4 us
  transfers between devices with their start and end apart: 5, of which 5 were waited for; matrix products, arithmetic and copies ran while one was open for 1% of the time, Pallas kernels for 0%

profile of v1, /device:TPU:2, one launch (start us, length us, event | category | flops | bytes accessed | tf_op | source)
XLA Modules:
  0.0 834.0 jit_solution(7665570716639026627)
XLA Ops:
  7.2 2.5 convolution_convert_fusion
  11.2 56.8 %all-gather.2.cloned.1.call-done = bf16[8192,512]{1,0:T(8,128)(2,1)} async-done(((bf16[512,512]{1,0:T(8,128)(2,1)}), bf16[8192,512]{1,0:T(8,128)(2,1)}) %all-gather.2.cloned.1.call-update) | async-done | bytes 8388624 | tf_op jit(solution)/shard_map/all_gather | solution.py:56
  68.0 80.6 %while.28 = (s32[]{:T(128)}, f32[512,512]{1,0:T(8,128)S(1)}, s32[1,16]{1,0:T(1,128)S(1)}, s32[1,512,16]{1,2,0:T(8,128)}, s32[1]{0:T(128)}, /*index=5*/bf16[8192,...) while((s32[]{:T(128)}, f32[512,512]{1,0:T(8,128)S(1)}, s32[1,16]{1,0:T(1,128)S(1)}, ...), condition=%wide.region_3.4_spmd.clone, body=%wide.region_1.3_spmd.clone.sunk | while | flops 269499936 | bytes 2659034 | solution.py:66
  71.4 1.6 convolution_add_fusion.4
  76.4 1.6 convolution_add_fusion.4
  86.5 1.6 convolution_add_fusion.4
  91.6 1.6 convolution_add_fusion.4
  106.7 1.6 convolution_add_fusion.4
  116.8 1.6 convolution_add_fusion.4
  121.8 1.6 convolution_add_fusion.4
  131.9 1.6 convolution_add_fusion.4
  136.9 1.6 convolution_add_fusion.4
  147.0 1.6 convolution_add_fusion.4
  148.7 3.0 fusion.15
  151.7 7.9 broadcast_in_dim.94
  159.6 67.3 %while.27 = (s32[]{:T(128)}, f32[8192,512]{1,0:T(8,128)}, s32[1,16]{1,0:T(1,128)S(1)}, s32[1,512,16]{1,2,0:T(8,128)S(1)}, s32[1]{0:T(128)}, /*index=5*/bf16[1,51...) while((s32[]{:T(128)}, f32[8192,512]{1,0:T(8,128)}, ...), condition=%wide.region_6.7_spmd, body=%wide.region_4.6_spmd.sunk | while | flops 269237792 | bytes 1610968 | solution.py:92
  195.9 1.6 fusion.37
  227.0 101.1 %reduce-scatter.3.cloned.1.call-done = f32[512,512]{1,0:T(8,128)} async-done(((f32[8192,512]{1,0:T(8,128)}), f32[512,512]{1,0:T(8,128)}) %reduce-scatter.3.cloned.1.call-update) | async-done | bytes 1048592 | tf_op jit(solution)/shard_map/reduce_scatter | solution.py:91
  329.6 200.2 %reduce-scatter.5.cloned.1.call-done = f32[32,512]{1,0:T(8,128)} async-done(((f32[512,512]{1,0:T(8,128)}), f32[32,512]{1,0:T(8,128)}) %reduce-scatter.5.cloned.1.call-update) | async-done | bytes 65552 | tf_op jit(solution)/shard_map/reduce_scatter | solution.py:102
  529.8 2.1 fusion.16
  532.0 162.2 %all-reduce.7.cloned.1.call-done = (f32[512,512]{0,1:T(8,128)}, f32[512,512]{1,0:T(8,128)}) async-done(((f32[512,512]{0,1:T(8,128)}, f32[512,512]{1,0:T(8,128)}), (f32[512,512]{0,1:T(8,128)}, f32[512,512]{1,0:T(8,128)})) %all-reduce.7.cloned.1.call-update) | async-done | bytes 2097168 | tf_op jit(solution)/shard_map/psum | solution.py:8
  695.4 1.7 convolution_convert_fusion.1
  697.2 125.4 %all-reduce.5.cloned.1.call-done = (f32[512,512]{0,1:T(8,128)}, f32[512,512]{1,0:T(8,128)}) async-done(((f32[512,512]{0,1:T(8,128)}, f32[512,512]{1,0:T(8,128)}), (f32[512,512]{0,1:T(8,128)}, f32[512,512]{1,0:T(8,128)})) %all-reduce.5.cloned.1.call-update) | async-done | bytes 2097168 | tf_op jit(solution)/shard_map/psum | solution.py:9
  825.2 2.3 broadcast_multiply_fusion
  (143 shorter events, 94.1 us)
Async XLA Ops:
  7.2 141.5 %copy-start = (bf16[512,512]{1,0:T(8,128)(2,1)S(1)}, bf16[512,512]{1,0:T(8,128)(2,1)}, u32[]{:S(2)}) copy-start(bf16[512,512]{1,0:T(8,128)(2,1)} %param.15) | copy-start | bytes 1572868
  7.2 60.8 %all-gather.2.cloned.1.call-start = ((), (), s32[]{:S(2)}) async-start(), calls=%async_computation.2 | async-start | bytes 8912896 | tf_op jit(solution)/shard_map/all_gather | solution.py:56
  9.7 318.3 %reduce-scatter.3.cloned.1.call-start = ((), (), s32[]{:S(2)}) async-start(), calls=%async_computation.3 | async-start | bytes 17825792 | tf_op jit(solution)/shard_map/reduce_scatter | solution.py:91
  148.6 10.9 %copy-start.1 = (s32[1,512,16]{1,2,0:T(8,128)S(1)}, s32[1,512,16]{1,2,0:T(8,128)}, u32[]{:S(2)}) copy-start(s32[1,512,16]{1,2,0:T(8,128)} %get-tuple-element.467) | copy-start | bytes 98308
  159.6 168.5 %copy-start.3 = (bf16[512,512]{1,0:T(8,128)(2,1)S(1)}, bf16[512,512]{1,0:T(8,128)(2,1)}, u32[]{:S(2)}) copy-start(bf16[512,512]{1,0:T(8,128)(2,1)} %param.13) | copy-start | bytes 1572868
  159.6 534.6 %copy-start.4 = (bf16[512,512]{1,0:T(8,128)(2,1)S(1)}, bf16[512,512]{1,0:T(8,128)(2,1)}, u32[]{:S(2)}) copy-start(bf16[512,512]{1,0:T(8,128)(2,1)} %param.19) | copy-start | bytes 1572868
  159.6 535.9 %copy-start.2 = (bf16[512,512]{1,0:T(8,128)(2,1)S(1)}, bf16[512,512]{1,0:T(8,128)(2,1)}, u32[]{:S(2)}) copy-start(bf16[512,512]{1,0:T(8,128)(2,1)} %param.14) | copy-start | bytes 1572868
  226.9 302.8 %reduce-scatter.5.cloned.1.call-start = ((), (), s32[]{:S(2)}) async-start(), calls=%async_computation.4 | async-start | bytes 1114112 | tf_op jit(solution)/shard_map/reduce_scatter | solution.py:102
  328.1 366.1 %all-reduce.7.cloned.1.call-start = ((), (), s32[]{:S(2)}) async-start(), calls=%async_computation.6 | async-start | bytes 4194304 | tf_op jit(solution)/shard_map/psum | solution.py:8
  531.9 290.6 %all-reduce.5.cloned.1.call-start = ((), (), s32[]{:S(2)}) async-start(), calls=%async_computation.5 | async-start | bytes 4194304 | tf_op jit(solution)/shard_map/psum | solution.py:9
Sparse Core Ops, SparseCore 0:
  10.4 57.5 all-gather.1
  227.0 100.9 reduce-scatter.2
  331.9 197.8 reduce-scatter.4
  532.9 161.2 all-reduce.6
  696.7 125.8 all-reduce.4
